TPU v7x, 512 devices: a whole 4x8x8 slice. The times are simulated.
512 devices in a mesh: gy: 32 (over x_hi, y, core), gx: 16 (over z, x_lo).
Axes of the slice: x: 4 (x_hi: 2, x_lo: 2; x = x_hi * 2 + x_lo), y: 8, z: 8, core: 2. Of those that a mesh axis runs over, the one named last changes fastest.
Arguments:
- patches: float32 [32, 16, 256, 256], P('gy', 'gx'), may hold values from -6 to 6
- w_query: float32 [2, 256, 256], replicated, may hold values from -0.375 to 0.375
- w_key: float32 [2, 256, 256], replicated, may hold values from -0.375 to 0.375
- w_value: float32 [2, 256, 256], replicated, may hold values from -0.375 to 0.375
- w_out: float32 [2, 256, 256], replicated, may hold values from -1.5 to 1.5
Outputs:
- embedded: float32 [32, 16, 256, 256], P('gy', 'gx')
All inputs are finite; a program needn't handle non-finite values.
Results may differ from a plain program's by a relative error of at most 0.0003.
Values sent between devices are 32-bit elements; how exact they have to be, the bound alone decides.
A program may use at most 64 MiB of HBM per device.

v0:
```python
import jax
import jax.numpy as jnp
from jax import lax
from jax.sharding import PartitionSpec as P

D = 256
LAYERS = 2


EPSILON = 1e-06
SHARPNESS = 16.0
SCORE_SHIFT = 32.0


def from_behind(block, axis, distance):
    devices = range(lax.axis_size(axis))
    route = [(i - distance, i) for i in devices if i - distance in devices]
    return lax.ppermute(block, axis, route)


def unitize(rows):
    scale = lax.rsqrt(jnp.mean(rows * rows, axis=-1, keepdims=True) + EPSILON)
    return rows * scale * rows.shape[-1] ** (-0.5)


def matmul(left, right):
    return jnp.dot(left, right, precision=lax.Precision.HIGHEST, preferred_element_type=jnp.float32)


def against(left, right):
    return lax.dot_general(
        left,
        right,
        (((1,), (1,)), ((), ())),
        precision=lax.Precision.HIGHEST,
        preferred_element_type=jnp.float32,
    )


def transposed(left, right):
    return lax.dot_general(
        left,
        right,
        (((0,), (0,)), ((), ())),
        precision=lax.Precision.HIGHEST,
        preferred_element_type=jnp.float32,
    )


def pack_tile(tile, wq_layer, wk_layer, wv_layer):
    return jnp.concatenate(
        [unitize(matmul(tile, wq_layer)), unitize(matmul(tile, wk_layer)), matmul(tile, wv_layer)],
        axis=1,
    )


def pair_weights(own_tile, far_tile, present):
    own_query = own_tile[:, :D]
    own_keys = own_tile[:, D : 2 * D]
    far_query = far_tile[:, :D]
    far_keys = far_tile[:, D : 2 * D]
    scores = against(own_query, far_keys) + against(own_keys, far_query)
    return jnp.exp(SHARPNESS * scores - SCORE_SHIFT) * present


def one_sided(own_tile, far_tile, present):
    weights = pair_weights(own_tile, far_tile, present)
    return (matmul(weights, far_tile[:, 2 * D :]), jnp.sum(weights, axis=1))


def two_sided(own_tile, far_tile, present):
    weights = pair_weights(own_tile, far_tile, present)
    own_numer = matmul(weights, far_tile[:, 2 * D :])
    own_total = jnp.sum(weights, axis=1)
    far_numer = transposed(weights, own_tile[:, 2 * D :])
    far_total = jnp.sum(weights, axis=0)
    return (own_numer, own_total, far_numer, far_total)


def layer_pass(field, wq_layer, wk_layer, wv_layer, wo_layer):
    packed = pack_tile(field, wq_layer, wk_layer, wv_layer)
    row_index = lax.axis_index("gy")
    col_index = lax.axis_index("gx")
    row_count = lax.axis_size("gy")
    col_count = lax.axis_size("gx")
    has_south = row_index + 1 < row_count
    has_east = col_index + 1 < col_count
    has_west = col_index >= 1
    south = from_behind(packed, "gy", -1)
    east, south_east = from_behind((packed, south), "gx", -1)
    south_west = from_behind(south, "gx", 1)
    numer, total = one_sided(packed, packed, jnp.float32(1.0))
    east_numer, east_total, owed_e_numer, owed_e_total = two_sided(
        packed, east, has_east.astype(jnp.float32)
    )
    south_numer, south_total, owed_s_numer, owed_s_total = two_sided(
        packed, south, has_south.astype(jnp.float32)
    )
    se_numer, se_total, owed_se_numer, owed_se_total = two_sided(
        packed, south_east, (has_south & has_east).astype(jnp.float32)
    )
    sw_numer, sw_total, owed_sw_numer, owed_sw_total = two_sided(
        packed, south_west, (has_south & has_west).astype(jnp.float32)
    )
    numer = numer + east_numer + south_numer + se_numer + sw_numer
    total = total + east_total + south_total + se_total + sw_total
    arrived = from_behind(
        (owed_sw_numer, owed_sw_total, owed_s_numer, owed_s_total, owed_se_numer, owed_se_total),
        "gy",
        1,
    )
    got_e_numer, got_e_total, diag_e_numer, diag_e_total = from_behind(
        (owed_e_numer, owed_e_total, arrived[4], arrived[5]), "gx", 1
    )
    diag_w_numer, diag_w_total = from_behind((arrived[0], arrived[1]), "gx", -1)
    numer = numer + arrived[2] + got_e_numer + diag_e_numer + diag_w_numer
    total = total + arrived[3] + got_e_total + diag_e_total + diag_w_total
    mixed = numer / total[:, None]
    return field + jax.nn.gelu(matmul(mixed, wo_layer), approximate=False)


def on_device(patches, w_query, w_key, w_value, w_out):
    field = patches[0, 0]
    for layer in range(LAYERS):
        field = layer_pass(field, w_query[layer], w_key[layer], w_value[layer], w_out[layer])
    return field[None, None]


def solution(mesh):
    in_specs = (P("gy", "gx", None, None), P(), P(), P(), P())
    out_specs = P("gy", "gx", None, None)
    return jax.shard_map(
        on_device, mesh=mesh, in_specs=in_specs, out_specs=out_specs, check_vma=False
    )
```

profile of v0, /device:TPU:245, one launch (start us, length us, event | category | flops | bytes accessed | tf_op | source)
XLA Modules:
  0.0 225.5 jit_solution(10685979341987693702)
XLA Ops:
  3.5 2.6 %collective-permute-start.1 = (f32[256,768]{0,1:T(8,128)S(1)}, f32[256,768]{0,1:T(8,128)S(1)}, u32[]{:S(2)}, u32[]{:S(2)}) collective-permute-start(f32[256,768]{0,1:T(8,128)S(1)} %pad_maximum_fusion), channel_id=1, source_target_pairs={{16,0},{32,16},{48,32},{64,48},{80,64},{96,80},{112,96},{128,112},... | collective-permute-start | bytes 2359304 | tf_op jit(solution)/shard_map/ppermute | solution.py:18
  6.1 1.9 collective-permute-start
  9.8 7.3 %collective-permute-done.1 = f32[256,768]{0,1:T(8,128)S(1)} collective-permute-done((f32[256,768]{0,1:T(8,128)S(1)}, f32[256,768]{0,1:T(8,128)S(1)}, u32[]{:S(2)}, u32[]{:S(2)}) %collective-permute-start.1) | collective-permute-done | bytes 786464 | tf_op jit(solution)/shard_map/ppermute | solution.py:18
  20.4 1.9 collective-permute-start.2
  22.3 4.0 %collective-permute-done = f32[256,768]{0,1:T(8,128)} collective-permute-done((f32[256,768]{0,1:T(8,128)S(1)}, f32[256,768]{0,1:T(8,128)}, u32[]{:S(2)}, u32[]{:S(2)}) %collective-permute-start) | collective-permute-done | bytes 786464 | tf_op jit(solution)/shard_map/ppermute | solution.py:18
  29.5 4.9 %collective-permute-start.11 = (f32[256]{0:T(256)S(1)}, f32[256]{0:T(256)S(1)}, u32[]{:S(2)}, u32[]{:S(2)}) collective-permute-start(f32[256]{0:T(256)S(1)} %get-tuple-element.14), channel_id=1, source_target_pairs={{0,1},{1,2},{2,3},{3,4},{4,5},{5,6},{6,7},{7,8},{8,9},{9,10},{10,1... | collective-permute-start | bytes 3080 | tf_op jit(solution)/shard_map/ppermute | solution.py:18
  34.5 3.4 %collective-permute-start.3 = (f32[256,768]{0,1:T(8,128)S(1)}, f32[256,768]{0,1:T(8,128)S(1)}, u32[]{:S(2)}, u32[]{:S(2)}) collective-permute-start(f32[256,768]{0,1:T(8,128)S(1)} %collective-permute-done.1), channel_id=1, source_target_pairs={{0,1},{1,2},{2,3},{3,4},{4,5},{5,6},{6,7},{7,8},{8,9},{9,10},{10,1... | collective-permute-start | bytes 2359304 | tf_op jit(solution)/shard_map/ppermute | solution.py:18
  40.0 20.0 %collective-permute-done.2 = f32[256,768]{0,1:T(8,128)S(1)} collective-permute-done((f32[256,768]{0,1:T(8,128)S(1)}, f32[256,768]{0,1:T(8,128)S(1)}, u32[]{:S(2)}, u32[]{:S(2)}) %collective-permute-start.2) | collective-permute-done | bytes 786464 | tf_op jit(solution)/shard_map/ppermute | solution.py:18
  61.3 12.3 %collective-permute-start.12 = (f32[256]{0:T(256)S(1)}, f32[256]{0:T(256)S(1)}, u32[]{:S(2)}, u32[]{:S(2)}) collective-permute-start(f32[256]{0:T(256)S(1)} %get-tuple-element.18), channel_id=1, source_target_pairs={{0,16},{16,32},{32,48},{48,64},{64,80},{80,96},{96,112},{112,128},... | collective-permute-start | bytes 3080 | tf_op jit(solution)/shard_map/ppermute | solution.py:18
  74.0 1.9 collective-permute-start.6
  77.7 2.1 collective-permute-start.8
  86.5 6.7 %collective-permute-start.5 = (f32[256,256]{1,0:T(8,128)S(1)}, f32[256,256]{1,0:T(8,128)S(1)}, u32[]{:S(2)}, u32[]{:S(2)}) collective-permute-start(f32[256,256]{1,0:T(8,128)S(1)} %fusion.149), channel_id=1, source_target_pairs={{0,1},{1,2},{2,3},{3,4},{4,5},{5,6},{6,7},{7,8},{8,9},{9,10},{10,1... | collective-permute-start | bytes 786440 | tf_op jit(solution)/shard_map/ppermute | solution.py:18
  95.1 3.4 %collective-permute-start.7 = (f32[256,256]{1,0:T(8,128)S(1)}, f32[256,256]{1,0:T(8,128)S(1)}, u32[]{:S(2)}, u32[]{:S(2)}) collective-permute-start(f32[256,256]{1,0:T(8,128)S(1)} %collective-permute-done.6), channel_id=1, source_target_pairs={{0,1},{1,2},{2,3},{3,4},{4,5},{5,6},{6,7},{7,8},{8,9},{9,10},{10,1... | collective-permute-start | bytes 786440 | tf_op jit(solution)/shard_map/ppermute | solution.py:18
  98.5 2.8 %collective-permute-start.9 = (f32[256,256]{1,0:T(8,128)S(1)}, f32[256,256]{1,0:T(8,128)S(1)}, u32[]{:S(2)}, u32[]{:S(2)}) collective-permute-start(f32[256,256]{1,0:T(8,128)S(1)} %collective-permute-done.8), channel_id=1, source_target_pairs={{1,0},{2,1},{3,2},{4,3},{5,4},{6,5},{7,6},{8,7},{9,8},{10,9},{11,1... | collective-permute-start | bytes 786440 | tf_op jit(solution)/shard_map/ppermute | solution.py:18
  102.0 3.0 %collective-permute-done.7 = f32[256,256]{1,0:T(8,128)S(1)} collective-permute-done((f32[256,256]{1,0:T(8,128)S(1)}, f32[256,256]{1,0:T(8,128)S(1)}, u32[]{:S(2)}, u32[]{:S(2)}) %collective-permute-start.7) | collective-permute-done | bytes 262176 | tf_op jit(solution)/shard_map/ppermute | solution.py:18
  104.9 6.8 %collective-permute-done.9 = f32[256,256]{1,0:T(8,128)S(1)} collective-permute-done((f32[256,256]{1,0:T(8,128)S(1)}, f32[256,256]{1,0:T(8,128)S(1)}, u32[]{:S(2)}, u32[]{:S(2)}) %collective-permute-start.9) | collective-permute-done | bytes 262176 | tf_op jit(solution)/shard_map/ppermute | solution.py:18
  115.8 2.4 %collective-permute-start.17 = (f32[256,768]{0,1:T(8,128)S(1)}, f32[256,768]{0,1:T(8,128)S(1)}, u32[]{:S(2)}, u32[]{:S(2)}) collective-permute-start(f32[256,768]{0,1:T(8,128)S(1)} %pad_maximum_fusion.1), channel_id=1, source_target_pairs={{16,0},{32,16},{48,32},{64,48},{80,64},{96,80},{112,96},{128,112},... | collective-permute-start | bytes 2359304 | tf_op jit(solution)/shard_map/ppermute | solution.py:18
  118.3 1.9 collective-permute-start.16
  122.0 7.4 %collective-permute-done.17 = f32[256,768]{0,1:T(8,128)S(1)} collective-permute-done((f32[256,768]{0,1:T(8,128)S(1)}, f32[256,768]{0,1:T(8,128)S(1)}, u32[]{:S(2)}, u32[]{:S(2)}) %collective-permute-start.17) | collective-permute-done | bytes 786464 | tf_op jit(solution)/shard_map/ppermute | solution.py:18
  134.6 3.6 %collective-permute-start.19 = (f32[256,768]{0,1:T(8,128)S(1)}, f32[256,768]{0,1:T(8,128)S(1)}, u32[]{:S(2)}, u32[]{:S(2)}) collective-permute-start(f32[256,768]{0,1:T(8,128)S(1)} %collective-permute-done.17), channel_id=1, source_target_pairs={{0,1},{1,2},{2,3},{3,4},{4,5},{5,6},{6,7},{7,8},{8,9},{9,10},{10,1... | collective-permute-start | bytes 2359304 | tf_op jit(solution)/shard_map/ppermute | solution.py:18
  140.7 30.4 %collective-permute-done.18 = f32[256,768]{0,1:T(8,128)S(1)} collective-permute-done((f32[256,768]{0,1:T(8,128)S(1)}, f32[256,768]{0,1:T(8,128)S(1)}, u32[]{:S(2)}, u32[]{:S(2)}) %collective-permute-start.18) | collective-permute-done | bytes 786464 | tf_op jit(solution)/shard_map/ppermute | solution.py:18
  172.4 8.5 %collective-permute-start.28 = (f32[256]{0:T(256)S(1)}, f32[256]{0:T(256)S(1)}, u32[]{:S(2)}, u32[]{:S(2)}) collective-permute-start(f32[256]{0:T(256)S(1)} %get-tuple-element.10), channel_id=1, source_target_pairs={{0,16},{16,32},{32,48},{48,64},{64,80},{80,96},{96,112},{112,128},... | collective-permute-start | bytes 3080 | tf_op jit(solution)/shard_map/ppermute | solution.py:18
  181.4 1.9 collective-permute-start.22
  187.4 1.9 collective-permute-start.27
  191.3 6.4 %collective-permute-start.29 = (f32[256]{0:T(256)S(1)}, f32[256]{0:T(256)S(1)}, u32[]{:S(2)}, u32[]{:S(2)}) collective-permute-start(f32[256]{0:T(256)S(1)} %collective-permute-done.28), channel_id=1, source_target_pairs={{0,1},{1,2},{2,3},{3,4},{4,5},{5,6},{6,7},{7,8},{8,9},{9,10},{10,1... | collective-permute-start | bytes 3080 | tf_op jit(solution)/shard_map/ppermute | solution.py:18
  198.1 2.2 collective-permute-start.20
  200.3 1.9 collective-permute-start.21
  202.3 4.3 %collective-permute-start.31 = (f32[256]{0:T(256)S(1)}, f32[256]{0:T(256)S(1)}, u32[]{:S(2)}, u32[]{:S(2)}) collective-permute-start(f32[256]{0:T(256)S(1)} %collective-permute-done.30), channel_id=1, source_target_pairs={{1,0},{2,1},{3,2},{4,3},{5,4},{6,5},{7,6},{8,7},{9,8},{10,9},{11,1... | collective-permute-start | bytes 3080 | tf_op jit(solution)/shard_map/ppermute | solution.py:18
  206.6 1.9 collective-permute-start.23
  208.5 4.3 %collective-permute-start.25 = (f32[256,256]{1,0:T(8,128)S(1)}, f32[256,256]{1,0:T(8,128)S(1)}, u32[]{:S(2)}, u32[]{:S(2)}) collective-permute-start(f32[256,256]{1,0:T(8,128)S(1)} %collective-permute-done.24), channel_id=1, source_target_pairs={{1,0},{2,1},{3,2},{4,3},{5,4},{6,5},{7,6},{8,7},{9,8},{10,9},{11,1... | collective-permute-start | bytes 786440 | tf_op jit(solution)/shard_map/ppermute | solution.py:18
  213.4 2.7 %collective-permute-done.23 = f32[256,256]{1,0:T(8,128)S(1)} collective-permute-done((f32[256,256]{1,0:T(8,128)S(1)}, f32[256,256]{1,0:T(8,128)S(1)}, u32[]{:S(2)}, u32[]{:S(2)}) %collective-permute-start.23) | collective-permute-done | bytes 262176 | tf_op jit(solution)/shard_map/ppermute | solution.py:18
  216.1 7.1 %collective-permute-done.25 = f32[256,256]{1,0:T(8,128)S(1)} collective-permute-done((f32[256,256]{1,0:T(8,128)S(1)}, f32[256,256]{1,0:T(8,128)S(1)}, u32[]{:S(2)}, u32[]{:S(2)}) %collective-permute-start.25) | collective-permute-done | bytes 262176 | tf_op jit(solution)/shard_map/ppermute | solution.py:18
  (101 shorter events, 50.7 us)
Async XLA Ops:
  3.5 13.7 %collective-permute-start.1 = (f32[256,768]{0,1:T(8,128)S(1)}, f32[256,768]{0,1:T(8,128)S(1)}, u32[]{:S(2)}, u32[]{:S(2)}) collective-permute-start(f32[256,768]{0,1:T(8,128)S(1)} %pad_maximum_fusion), channel_id=1, source_target_pairs={{16,0},{32,16},{48,32},{64,48},{80,64},{96,80},{112,96},{128,112},... | collective-permute-start | bytes 2359304 | tf_op jit(solution)/shard_map/ppermute | solution.py:18
  6.1 20.3 %collective-permute-start = (f32[256,768]{0,1:T(8,128)S(1)}, f32[256,768]{0,1:T(8,128)}, u32[]{:S(2)}, u32[]{:S(2)}) collective-permute-start(f32[256,768]{0,1:T(8,128)S(1)} %pad_maximum_fusion), channel_id=1, source_target_pairs={{1,0},{2,1},{3,2},{4,3},{5,4},{6,5},{7,6},{8,7},{9,8},{10,9},{11,1... | collective-permute-start | bytes 2359304 | tf_op jit(solution)/shard_map/ppermute | solution.py:18
  18.5 61.8 %collective-permute-start.10 = (f32[256]{0:T(256)S(1)}, f32[256]{0:T(256)S(1)}, u32[]{:S(2)}, u32[]{:S(2)}) collective-permute-start(f32[256]{0:T(256)S(1)} %get-tuple-element.16), channel_id=1, source_target_pairs={{0,16},{16,32},{32,48},{48,64},{64,80},{80,96},{96,112},{112,128},... | collective-permute-start | bytes 3080 | tf_op jit(solution)/shard_map/ppermute | solution.py:18
  20.4 39.6 %collective-permute-start.2 = (f32[256,768]{0,1:T(8,128)S(1)}, f32[256,768]{0,1:T(8,128)S(1)}, u32[]{:S(2)}, u32[]{:S(2)}) collective-permute-start(f32[256,768]{0,1:T(8,128)S(1)} %collective-permute-done.1), channel_id=1, source_target_pairs={{1,0},{2,1},{3,2},{4,3},{5,4},{6,5},{7,6},{8,7},{9,8},{10,9},{11,1... | collective-permute-start | bytes 2359304 | tf_op jit(solution)/shard_map/ppermute | solution.py:18
  29.5 55.0 %collective-permute-start.11 = (f32[256]{0:T(256)S(1)}, f32[256]{0:T(256)S(1)}, u32[]{:S(2)}, u32[]{:S(2)}) collective-permute-start(f32[256]{0:T(256)S(1)} %get-tuple-element.14), channel_id=1, source_target_pairs={{0,1},{1,2},{2,3},{3,4},{4,5},{5,6},{6,7},{7,8},{8,9},{9,10},{10,1... | collective-permute-start | bytes 3080 | tf_op jit(solution)/shard_map/ppermute | solution.py:18
  34.5 41.5 %collective-permute-start.3 = (f32[256,768]{0,1:T(8,128)S(1)}, f32[256,768]{0,1:T(8,128)S(1)}, u32[]{:S(2)}, u32[]{:S(2)}) collective-permute-start(f32[256,768]{0,1:T(8,128)S(1)} %collective-permute-done.1), channel_id=1, source_target_pairs={{0,1},{1,2},{2,3},{3,4},{4,5},{5,6},{6,7},{7,8},{8,9},{9,10},{10,1... | collective-permute-start | bytes 2359304 | tf_op jit(solution)/shard_map/ppermute | solution.py:18
  61.3 20.9 %collective-permute-start.12 = (f32[256]{0:T(256)S(1)}, f32[256]{0:T(256)S(1)}, u32[]{:S(2)}, u32[]{:S(2)}) collective-permute-start(f32[256]{0:T(256)S(1)} %get-tuple-element.18), channel_id=1, source_target_pairs={{0,16},{16,32},{32,48},{48,64},{64,80},{80,96},{96,112},{112,128},... | collective-permute-start | bytes 3080 | tf_op jit(solution)/shard_map/ppermute | solution.py:18
  74.0 21.1 %collective-permute-start.6 = (f32[256,256]{1,0:T(8,128)S(1)}, f32[256,256]{1,0:T(8,128)S(1)}, u32[]{:S(2)}, u32[]{:S(2)}) collective-permute-start(f32[256,256]{1,0:T(8,128)S(1)} %fusion.150), channel_id=1, source_target_pairs={{0,16},{16,32},{32,48},{48,64},{64,80},{80,96},{96,112},{112,128},... | collective-permute-start | bytes 786440 | tf_op jit(solution)/shard_map/ppermute | solution.py:18
  77.7 20.8 %collective-permute-start.8 = (f32[256,256]{1,0:T(8,128)S(1)}, f32[256,256]{1,0:T(8,128)S(1)}, u32[]{:S(2)}, u32[]{:S(2)}) collective-permute-start(f32[256,256]{1,0:T(8,128)S(1)} %fusion.151), channel_id=1, source_target_pairs={{0,16},{16,32},{32,48},{48,64},{64,80},{80,96},{96,112},{112,128},... | collective-permute-start | bytes 786440 | tf_op jit(solution)/shard_map/ppermute | solution.py:18
  80.2 6.2 %collective-permute-start.14 = (f32[256]{0:T(256)S(1)}, f32[256]{0:T(256)S(1)}, u32[]{:S(2)}, u32[]{:S(2)}) collective-permute-start(f32[256]{0:T(256)S(1)} %get-tuple-element.20), channel_id=1, source_target_pairs={{0,16},{16,32},{32,48},{48,64},{64,80},{80,96},{96,112},{112,128},... | collective-permute-start | bytes 3080 | tf_op jit(solution)/shard_map/ppermute | solution.py:18
  82.2 11.0 %collective-permute-start.13 = (f32[256]{0:T(256)S(1)}, f32[256]{0:T(256)S(1)}, u32[]{:S(2)}, u32[]{:S(2)}) collective-permute-start(f32[256]{0:T(256)S(1)} %collective-permute-done.12), channel_id=1, source_target_pairs={{0,1},{1,2},{2,3},{3,4},{4,5},{5,6},{6,7},{7,8},{8,9},{9,10},{10,1... | collective-permute-start | bytes 3080 | tf_op jit(solution)/shard_map/ppermute | solution.py:18
  84.5 17.4 %collective-permute-start.4 = (f32[256,256]{1,0:T(8,128)S(1)}, f32[256,256]{1,0:T(8,128)S(1)}, u32[]{:S(2)}, u32[]{:S(2)}) collective-permute-start(f32[256,256]{1,0:T(8,128)S(1)} %fusion.148), channel_id=1, source_target_pairs={{0,16},{16,32},{32,48},{48,64},{64,80},{80,96},{96,112},{112,128},... | collective-permute-start | bytes 786440 | tf_op jit(solution)/shard_map/ppermute | solution.py:18
  86.5 15.5 %collective-permute-start.5 = (f32[256,256]{1,0:T(8,128)S(1)}, f32[256,256]{1,0:T(8,128)S(1)}, u32[]{:S(2)}, u32[]{:S(2)}) collective-permute-start(f32[256,256]{1,0:T(8,128)S(1)} %fusion.149), channel_id=1, source_target_pairs={{0,1},{1,2},{2,3},{3,4},{4,5},{5,6},{6,7},{7,8},{8,9},{9,10},{10,1... | collective-permute-start | bytes 786440 | tf_op jit(solution)/shard_map/ppermute | solution.py:18
  93.2 8.8 %collective-permute-start.15 = (f32[256]{0:T(256)S(1)}, f32[256]{0:T(256)S(1)}, u32[]{:S(2)}, u32[]{:S(2)}) collective-permute-start(f32[256]{0:T(256)S(1)} %collective-permute-done.14), channel_id=1, source_target_pairs={{1,0},{2,1},{3,2},{4,3},{5,4},{6,5},{7,6},{8,7},{9,8},{10,9},{11,1... | collective-permute-start | bytes 3080 | tf_op jit(solution)/shard_map/ppermute | solution.py:18
  95.1 9.8 %collective-permute-start.7 = (f32[256,256]{1,0:T(8,128)S(1)}, f32[256,256]{1,0:T(8,128)S(1)}, u32[]{:S(2)}, u32[]{:S(2)}) collective-permute-start(f32[256,256]{1,0:T(8,128)S(1)} %collective-permute-done.6), channel_id=1, source_target_pairs={{0,1},{1,2},{2,3},{3,4},{4,5},{5,6},{6,7},{7,8},{8,9},{9,10},{10,1... | collective-permute-start | bytes 786440 | tf_op jit(solution)/shard_map/ppermute | solution.py:18
  98.5 13.3 %collective-permute-start.9 = (f32[256,256]{1,0:T(8,128)S(1)}, f32[256,256]{1,0:T(8,128)S(1)}, u32[]{:S(2)}, u32[]{:S(2)}) collective-permute-start(f32[256,256]{1,0:T(8,128)S(1)} %collective-permute-done.8), channel_id=1, source_target_pairs={{1,0},{2,1},{3,2},{4,3},{5,4},{6,5},{7,6},{8,7},{9,8},{10,9},{11,1... | collective-permute-start | bytes 786440 | tf_op jit(solution)/shard_map/ppermute | solution.py:18
  115.8 13.6 %collective-permute-start.17 = (f32[256,768]{0,1:T(8,128)S(1)}, f32[256,768]{0,1:T(8,128)S(1)}, u32[]{:S(2)}, u32[]{:S(2)}) collective-permute-start(f32[256,768]{0,1:T(8,128)S(1)} %pad_maximum_fusion.1), channel_id=1, source_target_pairs={{16,0},{32,16},{48,32},{64,48},{80,64},{96,80},{112,96},{128,112},... | collective-permute-start | bytes 2359304 | tf_op jit(solution)/shard_map/ppermute | solution.py:18
  118.3 19.9 %collective-permute-start.16 = (f32[256,768]{0,1:T(8,128)S(1)}, f32[256,768]{0,1:T(8,128)S(1)}, u32[]{:S(2)}, u32[]{:S(2)}) collective-permute-start(f32[256,768]{0,1:T(8,128)S(1)} %pad_maximum_fusion.1), channel_id=1, source_target_pairs={{1,0},{2,1},{3,2},{4,3},{5,4},{6,5},{7,6},{8,7},{9,8},{10,9},{11,1... | collective-permute-start | bytes 2359304 | tf_op jit(solution)/shard_map/ppermute | solution.py:18
  130.7 58.6 %collective-permute-start.26 = (f32[256]{0:T(256)S(1)}, f32[256]{0:T(256)S(1)}, u32[]{:S(2)}, u32[]{:S(2)}) collective-permute-start(f32[256]{0:T(256)S(1)} %get-tuple-element.8), channel_id=1, source_target_pairs={{0,16},{16,32},{32,48},{48,64},{64,80},{80,96},{96,112},{112,128},... | collective-permute-start | bytes 3080 | tf_op jit(solution)/shard_map/ppermute | solution.py:18
  132.7 38.5 %collective-permute-start.18 = (f32[256,768]{0,1:T(8,128)S(1)}, f32[256,768]{0,1:T(8,128)S(1)}, u32[]{:S(2)}, u32[]{:S(2)}) collective-permute-start(f32[256,768]{0,1:T(8,128)S(1)} %collective-permute-done.17), channel_id=1, source_target_pairs={{1,0},{2,1},{3,2},{4,3},{5,4},{6,5},{7,6},{8,7},{9,8},{10,9},{11,1... | collective-permute-start | bytes 2359304 | tf_op jit(solution)/shard_map/ppermute | solution.py:18
  134.6 48.7 %collective-permute-start.19 = (f32[256,768]{0,1:T(8,128)S(1)}, f32[256,768]{0,1:T(8,128)S(1)}, u32[]{:S(2)}, u32[]{:S(2)}) collective-permute-start(f32[256,768]{0,1:T(8,128)S(1)} %collective-permute-done.17), channel_id=1, source_target_pairs={{0,1},{1,2},{2,3},{3,4},{4,5},{5,6},{6,7},{7,8},{8,9},{9,10},{10,1... | collective-permute-start | bytes 2359304 | tf_op jit(solution)/shard_map/ppermute | solution.py:18
  172.4 18.8 %collective-permute-start.28 = (f32[256]{0:T(256)S(1)}, f32[256]{0:T(256)S(1)}, u32[]{:S(2)}, u32[]{:S(2)}) collective-permute-start(f32[256]{0:T(256)S(1)} %get-tuple-element.10), channel_id=1, source_target_pairs={{0,16},{16,32},{32,48},{48,64},{64,80},{80,96},{96,112},{112,128},... | collective-permute-start | bytes 3080 | tf_op jit(solution)/shard_map/ppermute | solution.py:18
  181.4 25.1 %collective-permute-start.22 = (f32[256,256]{1,0:T(8,128)S(1)}, f32[256,256]{1,0:T(8,128)S(1)}, u32[]{:S(2)}, u32[]{:S(2)}) collective-permute-start(f32[256,256]{1,0:T(8,128)S(1)} %fusion.156), channel_id=1, source_target_pairs={{0,16},{16,32},{32,48},{48,64},{64,80},{80,96},{96,112},{112,128},... | collective-permute-start | bytes 786440 | tf_op jit(solution)/shard_map/ppermute | solution.py:18
  185.1 23.4 %collective-permute-start.24 = (f32[256,256]{1,0:T(8,128)S(1)}, f32[256,256]{1,0:T(8,128)S(1)}, u32[]{:S(2)}, u32[]{:S(2)}) collective-permute-start(f32[256,256]{1,0:T(8,128)S(1)} %fusion.157), channel_id=1, source_target_pairs={{0,16},{16,32},{32,48},{48,64},{64,80},{80,96},{96,112},{112,128},... | collective-permute-start | bytes 786440 | tf_op jit(solution)/shard_map/ppermute | solution.py:18
  187.4 10.7 %collective-permute-start.27 = (f32[256]{0:T(256)S(1)}, f32[256]{0:T(256)S(1)}, u32[]{:S(2)}, u32[]{:S(2)}) collective-permute-start(f32[256]{0:T(256)S(1)} %get-tuple-element.6), channel_id=1, source_target_pairs={{0,1},{1,2},{2,3},{3,4},{4,5},{5,6},{6,7},{7,8},{8,9},{9,10},{10,1... | collective-permute-start | bytes 3080 | tf_op jit(solution)/shard_map/ppermute | solution.py:18
  189.3 11.0 %collective-permute-start.30 = (f32[256]{0:T(256)S(1)}, f32[256]{0:T(256)S(1)}, u32[]{:S(2)}, u32[]{:S(2)}) collective-permute-start(f32[256]{0:T(256)S(1)} %get-tuple-element.12), channel_id=1, source_target_pairs={{0,16},{16,32},{32,48},{48,64},{64,80},{80,96},{96,112},{112,128},... | collective-permute-start | bytes 3080 | tf_op jit(solution)/shard_map/ppermute | solution.py:18
  191.3 11.0 %collective-permute-start.29 = (f32[256]{0:T(256)S(1)}, f32[256]{0:T(256)S(1)}, u32[]{:S(2)}, u32[]{:S(2)}) collective-permute-start(f32[256]{0:T(256)S(1)} %collective-permute-done.28), channel_id=1, source_target_pairs={{0,1},{1,2},{2,3},{3,4},{4,5},{5,6},{6,7},{7,8},{8,9},{9,10},{10,1... | collective-permute-start | bytes 3080 | tf_op jit(solution)/shard_map/ppermute | solution.py:18
  198.1 15.3 %collective-permute-start.20 = (f32[256,256]{1,0:T(8,128)S(1)}, f32[256,256]{1,0:T(8,128)S(1)}, u32[]{:S(2)}, u32[]{:S(2)}) collective-permute-start(f32[256,256]{1,0:T(8,128)S(1)} %fusion.154), channel_id=1, source_target_pairs={{0,16},{16,32},{32,48},{48,64},{64,80},{80,96},{96,112},{112,128},... | collective-permute-start | bytes 786440 | tf_op jit(solution)/shard_map/ppermute | solution.py:18
  200.3 13.1 %collective-permute-start.21 = (f32[256,256]{1,0:T(8,128)S(1)}, f32[256,256]{1,0:T(8,128)S(1)}, u32[]{:S(2)}, u32[]{:S(2)}) collective-permute-start(f32[256,256]{1,0:T(8,128)S(1)} %fusion.155), channel_id=1, source_target_pairs={{0,1},{1,2},{2,3},{3,4},{4,5},{5,6},{6,7},{7,8},{8,9},{9,10},{10,1... | collective-permute-start | bytes 786440 | tf_op jit(solution)/shard_map/ppermute | solution.py:18
  202.3 11.1 %collective-permute-start.31 = (f32[256]{0:T(256)S(1)}, f32[256]{0:T(256)S(1)}, u32[]{:S(2)}, u32[]{:S(2)}) collective-permute-start(f32[256]{0:T(256)S(1)} %collective-permute-done.30), channel_id=1, source_target_pairs={{1,0},{2,1},{3,2},{4,3},{5,4},{6,5},{7,6},{8,7},{9,8},{10,9},{11,1... | collective-permute-start | bytes 3080 | tf_op jit(solution)/shard_map/ppermute | solution.py:18
  206.6 9.6 %collective-permute-start.23 = (f32[256,256]{1,0:T(8,128)S(1)}, f32[256,256]{1,0:T(8,128)S(1)}, u32[]{:S(2)}, u32[]{:S(2)}) collective-permute-start(f32[256,256]{1,0:T(8,128)S(1)} %collective-permute-done.22), channel_id=1, source_target_pairs={{0,1},{1,2},{2,3},{3,4},{4,5},{5,6},{6,7},{7,8},{8,9},{9,10},{10,1... | collective-permute-start | bytes 786440 | tf_op jit(solution)/shard_map/ppermute | solution.py:18
  208.5 14.7 %collective-permute-start.25 = (f32[256,256]{1,0:T(8,128)S(1)}, f32[256,256]{1,0:T(8,128)S(1)}, u32[]{:S(2)}, u32[]{:S(2)}) collective-permute-start(f32[256,256]{1,0:T(8,128)S(1)} %collective-permute-done.24), channel_id=1, source_target_pairs={{1,0},{2,1},{3,2},{4,3},{5,4},{6,5},{7,6},{8,7},{9,8},{10,9},{11,1... | collective-permute-start | bytes 786440 | tf_op jit(solution)/shard_map/ppermute | solution.py:18
  (6 other events, 17.1 us)
where the time goes:
time: 227 us; the launch traced here: 225 us
  starting transfers between devices  102 us (45%)
  waiting for transfers between devices  88.8 us (39%)
  matrix products  32.2 us (14%)
    ppermute x32, starting transfers between devices, from_behind(): return lax.ppermute(block, axis, route)  102 us
    ppermute x32, waiting for transfers between devices, from_behind(): return lax.ppermute(block, axis, route)  88.8 us
    dot_general x20, matrix products, against(): lax.dot_general(left, right, (((1,), (1,)), ((), ())), precision=lax.Prec...  14.6 us
    dot_general x18, matrix products, matmul(): jnp.dot(left, right, precision=lax.Precision.HIGHEST, preferred_element_t...  14.3 us
  transfers between devices with their start and end apart: 32, of which 9 were waited for; matrix products, arithmetic and copies ran while one was open for 10% of the time, Pallas kernels for 0%

commit v1 on v0

v1 whole, which is shorter than its diff:
```python
import functools

import jax
import jax.numpy as jnp
from jax import lax
from jax.experimental import pallas as pl
from jax.experimental.pallas import tpu as pltpu
from jax.sharding import PartitionSpec as P

D = 256
ROWS = 256
LAYERS = 2
CHUNKS = 2
CROWS = ROWS // CHUNKS
EPSILON = 1e-06
SCORE_SHIFT = 32.0
MESH = pl.DeviceIdType.MESH

OWN, NEAR, FAR = 0, 1, 2
NORTH, MID, SOUTH = 0, 1, 2

F32 = jnp.float32
BF16 = jnp.bfloat16


def split(x):
    hi = x.astype(BF16)
    return hi, (x - hi.astype(F32)).astype(BF16)


def dot(a, b, dims):
    return lax.dot_general(a, b, (dims, ((), ())), preferred_element_type=F32)


def dot3(a, b, dims):
    a_hi, a_lo = a
    b_hi, b_lo = b
    return dot(a_hi, b_hi, dims) + (dot(a_lo, b_hi, dims) + dot(a_hi, b_lo, dims))


NN = ((1,), (0,))
NT = ((1,), (1,))


def kernel(ny, nx, p_ref, wq_ref, wk_ref, wv_ref, wo_ref, o_ref,
           field, halo, norms, wq, wk, wv, wo, g_hi, g_lo, acc, tot,
           send_sem, recv_sem, load_sem):
    gy = lax.axis_index("gy")
    gx = lax.axis_index("gx")
    side = lax.rem(gx, 2)
    partner = gx + 1 - 2 * side
    onward = gx + 2 - 4 * side
    behind = gx - 2 + 4 * side
    has_onward = (onward >= 0) & (onward < nx)
    has_far = (behind >= 0) & (behind < nx)
    has_north = gy >= 1
    has_south = gy + 1 < ny

    loads = [pltpu.make_async_copy(p_ref, field.at[0], load_sem.at[0])]
    for n, (src, dst) in enumerate(((wq_ref, wq), (wk_ref, wk), (wv_ref, wv), (wo_ref, wo))):
        loads.append(pltpu.make_async_copy(src, dst, load_sem.at[n + 1]))
    for load in loads:
        load.start()

    barrier = pltpu.get_barrier_semaphore()

    def greet(y, x):
        pl.semaphore_signal(barrier, inc=1, device_id=(y, x), device_id_type=MESH)

    greet(gy, partner)
    pl.when(has_onward)(lambda: greet(gy, onward))
    pl.when(has_far)(lambda: greet(gy, behind))
    pl.when(has_north)(lambda: greet(gy - 1, gx))
    pl.when(has_south)(lambda: greet(gy + 1, gx))
    greetings = (1 + has_onward.astype(jnp.int32) + has_far.astype(jnp.int32)
                 + has_north.astype(jnp.int32) + has_south.astype(jnp.int32))
    loads[0].wait()
    pl.semaphore_wait(barrier, greetings)

    def rows(c):
        return pl.ds(c * CROWS, CROWS)

    def piece(layer, row, col, c, source=False):
        slot = row * 3 + col
        if c == CHUNKS:
            return norms.at[layer, slot]
        if source and row == MID and col == OWN:
            return field.at[layer, rows(c)]
        return halo.at[layer, slot, rows(c)]

    def sends():
        yield 0, OWN, MID, NEAR, (gy, partner), None
        yield 1, NEAR, MID, FAR, (gy, onward), has_onward
        for col in (OWN, NEAR, FAR):
            there = None if col != FAR else has_far
            yield 2 + col, col, SOUTH, col, (gy - 1, gx), has_north if there is None else has_north & there
            yield 5 + col, col, NORTH, col, (gy + 1, gx), has_south if there is None else has_south & there

    def copy(layer, send, c):
        kind, src_col, row, col, device, _ = send
        return pltpu.make_async_remote_copy(
            src_ref=piece(layer, MID, src_col, c, True),
            dst_ref=piece(layer, row, col, c),
            send_sem=send_sem.at[layer, kind, c],
            recv_sem=recv_sem.at[layer, row * 3 + col, c],
            device_id=device,
            device_id_type=MESH,
        )

    def guarded(condition, action):
        if condition is None:
            action()
        else:
            pl.when(condition)(action)

    plan = list(sends())

    def start(layer, src_col, c):
        for send in plan:
            if send[1] == src_col:
                guarded(send[5], lambda send=send: copy(layer, send, c).start())

    def arrival(layer, row, col, c):
        for send in plan:
            if send[2] == row and send[3] == col:
                copy(layer, send, c).wait_recv()

    def process(layer, row, col):
        slot = row * 3 + col
        tile = split(field[layer] if slot == 3 * MID + OWN else halo[layer, slot])
        n_rows = norms[layer, slot]
        both = dot3((g_hi[...], g_lo[...]), tile, NT)
        score = both[:ROWS] * n_rows[1:2] + both[ROWS:] * n_rows[0:1]
        weight = jnp.exp(score - SCORE_SHIFT)
        tot[...] += jnp.sum(weight, axis=1, keepdims=True)
        acc[...] += dot3(split(weight), tile, NN)

    def await_and_process(layer, row, col):
        def run():
            for c in range(CHUNKS + 1):
                arrival(layer, row, col, c)
            process(layer, row, col)
        conditions = {NORTH: has_north, SOUTH: has_south}[row]
        if col == FAR:
            conditions = conditions & has_far
        pl.when(conditions)(run)

    def layer_pass(layer, carry):
        for c in range(CHUNKS):
            start(layer, OWN, c)

        @pl.when(layer == 0)
        def _():
            for load in loads[1:]:
                load.wait()

        own = split(field[layer])
        wq_s = split(wq[layer])
        wk_s = split(wk[layer])
        query = dot3(own, wq_s, NN)
        keys = dot3(own, wk_s, NN)
        ones = jnp.ones((8, D), F32)

        def along_lanes(raw):
            total = lax.dot_general(ones, raw * raw, (NT, ((), ())),
                                    precision=lax.Precision.HIGHEST, preferred_element_type=F32)
            return lax.rsqrt(total * (1.0 / D) + EPSILON)

        first = lax.broadcasted_iota(jnp.int32, (8, ROWS), 0) == 0
        norms[layer, MID * 3 + OWN] = jnp.where(first, along_lanes(query), along_lanes(keys))
        start(layer, OWN, CHUNKS)

        def unitize(raw):
            scale = lax.rsqrt(jnp.mean(raw * raw, axis=-1, keepdims=True) + EPSILON)
            return raw * scale * D ** (-0.5)

        g1 = split(dot3(split(unitize(query)), wk_s, NT))
        g2 = split(dot3(split(unitize(keys)), wq_s, NT))
        g_hi[:ROWS] = g1[0]
        g_lo[:ROWS] = g1[1]
        g_hi[ROWS:] = g2[0]
        g_lo[ROWS:] = g2[1]
        acc[...] = jnp.zeros_like(acc)
        tot[...] = jnp.zeros_like(tot)
        process(layer, MID, OWN)

        for c in range(CHUNKS + 1):
            arrival(layer, MID, NEAR, c)
            start(layer, NEAR, c)
        process(layer, MID, NEAR)
        await_and_process(layer, NORTH, OWN)
        await_and_process(layer, SOUTH, OWN)

        @pl.when(has_far)
        def _():
            for c in range(CHUNKS + 1):
                arrival(layer, MID, FAR, c)
                start(layer, FAR, c)
            process(layer, MID, FAR)

        for col in (NEAR, FAR):
            for row in (NORTH, SOUTH):
                await_and_process(layer, row, col)

        mean = acc[...] * (1.0 / tot[...])
        mixed = dot3(split(mean), split(wv[layer]), NN)
        pre = dot3(split(mixed), split(wo[layer]), NN)
        field[layer + 1] = field[layer] + 0.5 * pre * (1.0 + lax.erf(pre * 0.5 ** 0.5))
        return carry

    lax.fori_loop(0, LAYERS, layer_pass, 0)
    o_ref[...] = field[LAYERS]

    def drain(layer, carry):
        for send in plan:
            for c in range(CHUNKS + 1):
                guarded(send[5], lambda send=send, c=c: copy(layer, send, c).wait_send())
        return carry

    lax.fori_loop(0, LAYERS, drain, 0)


def on_device(ny, nx, patches, w_query, w_key, w_value, w_out):
    any_space = pl.BlockSpec(memory_space=pl.ANY)
    weight = pltpu.VMEM((LAYERS, D, D), F32)
    out = pl.pallas_call(
        functools.partial(kernel, ny, nx),
        out_shape=jax.ShapeDtypeStruct((ROWS, D), F32),
        in_specs=[any_space] * 5,
        out_specs=pl.BlockSpec(memory_space=pltpu.VMEM),
        scratch_shapes=[
            pltpu.VMEM((LAYERS + 1, ROWS, D), F32),
            pltpu.VMEM((LAYERS, 9, ROWS, D), F32),
            pltpu.VMEM((LAYERS, 9, 8, ROWS), F32),
            weight, weight, weight, weight,
            pltpu.VMEM((2 * ROWS, D), BF16),
            pltpu.VMEM((2 * ROWS, D), BF16),
            pltpu.VMEM((ROWS, D), F32),
            pltpu.VMEM((ROWS, 1), F32),
            pltpu.SemaphoreType.DMA((LAYERS, 8, CHUNKS + 1)),
            pltpu.SemaphoreType.DMA((LAYERS, 9, CHUNKS + 1)),
            pltpu.SemaphoreType.DMA((5,)),
        ],
        compiler_params=pltpu.CompilerParams(
            collective_id=0, has_side_effects=True, vmem_limit_bytes=48 * 1024 * 1024
        ),
    )(patches[0, 0], w_query, w_key, w_value, w_out)
    return out[None, None]


def solution(mesh):
    in_specs = (P("gy", "gx", None, None), P(), P(), P(), P())
    out_specs = P("gy", "gx", None, None)
    return jax.shard_map(
        functools.partial(on_device, mesh.shape["gy"], mesh.shape["gx"]),
        mesh=mesh, in_specs=in_specs, out_specs=out_specs, check_vma=False
    )
```

time: 227 us -> 58.6 us (0.26)
  the two profiles are of different devices: /device:TPU:245 before, /device:TPU:136 now
where the time goes in v1:
time: 58.6 us; the launch traced here: 58.3 us
  Pallas kernels  52.4 us (89%)
  local copies, waits for them, and re-layouts  5.82 us (10%)
    pallas_call x1, Pallas kernels, on_device(): pl.pallas_call(functools.partial(kernel, ny, nx), out_shape=jax.ShapeDtyp...  52.4 us
    unnamed x11, local copies, waits for them, and re-layouts  5.82 us

profile of v1, /device:TPU:136, one launch (start us, length us, event | category | flops | bytes accessed | tf_op | source)
XLA Modules:
  0.0 58.3 jit_solution(4209913091583458212)
XLA Ops:
  0.0 0.0 copy-start
  0.0 1.0 %copy-done = f32[2,256,256]{2,1,0:T(8,128)S(1)} copy-done((f32[2,256,256]{2,1,0:T(8,128)S(1)}, f32[2,256,256]{2,1,0:T(8,128)}, u32[]{:S(2)}) %copy-start) | copy-done | bytes 524312
  1.0 0.0 copy-start.1
  1.0 1.0 %copy-done.1 = f32[2,256,256]{2,1,0:T(8,128)S(1)} copy-done((f32[2,256,256]{2,1,0:T(8,128)S(1)}, f32[2,256,256]{2,1,0:T(8,128)}, u32[]{:S(2)}) %copy-start.1) | copy-done | bytes 524312
  2.1 0.0 copy-start.2
  2.1 1.0 %copy-done.2 = f32[2,256,256]{2,1,0:T(8,128)S(1)} copy-done((f32[2,256,256]{2,1,0:T(8,128)S(1)}, f32[2,256,256]{2,1,0:T(8,128)}, u32[]{:S(2)}) %copy-start.2) | copy-done | bytes 524312
  3.1 0.0 copy-start.3
  3.1 1.0 %copy-done.3 = f32[2,256,256]{2,1,0:T(8,128)S(1)} copy-done((f32[2,256,256]{2,1,0:T(8,128)S(1)}, f32[2,256,256]{2,1,0:T(8,128)}, u32[]{:S(2)}) %copy-start.3) | copy-done | bytes 524312
  4.2 0.0 copy-start.4
  4.2 0.9 %copy-done.4 = f32[1,1,256,256]{3,2,1,0:T(8,128)S(1)} copy-done((f32[1,1,256,256]{3,2,1,0:T(8,128)S(1)}, f32[1,1,256,256]{3,2,1,0:T(8,128)}, u32[]{:S(2)}) %copy-start.4) | copy-done | bytes 262168
  5.1 52.4 %shard_map.55 = f32[256,256]{1,0:T(8,128)S(1)} custom-call(f32[256,256]{1,0:T(8,128)S(1)} %bitcast.3, f32[2,256,256]{2,1,0:T(8,128)S(1)} %copy-done, f32[2,256,256]{2,1,0:T(8,128)S(1)} %copy-done.1, f32[2,256,256]{2,1,0:T(8,128)S(1)} %copy-done.2, f32[2,256,256]{2,1,0:T(8,128)S(1)} %copy-done.3), custom_call_target="tpu_custom_call" | custom-call | tf_op jit(solution)/shard_map/pallas_call | solution.py:226
  57.6 0.7 %copy.7 = f32[1,1,256,256]{3,2,1,0:T(8,128)} copy(f32[1,1,256,256]{3,2,1,0:T(8,128)S(1)} %bitcast.2) | data formatting | bytes 524288
Async XLA Ops:
  0.0 1.0 %copy-start = (f32[2,256,256]{2,1,0:T(8,128)S(1)}, f32[2,256,256]{2,1,0:T(8,128)}, u32[]{:S(2)}) copy-start(f32[2,256,256]{2,1,0:T(8,128)} %wq_ref.1) | copy-start | bytes 1572868
  1.0 1.0 %copy-start.1 = (f32[2,256,256]{2,1,0:T(8,128)S(1)}, f32[2,256,256]{2,1,0:T(8,128)}, u32[]{:S(2)}) copy-start(f32[2,256,256]{2,1,0:T(8,128)} %wk_ref.1) | copy-start | bytes 1572868
  2.1 1.0 %copy-start.2 = (f32[2,256,256]{2,1,0:T(8,128)S(1)}, f32[2,256,256]{2,1,0:T(8,128)}, u32[]{:S(2)}) copy-start(f32[2,256,256]{2,1,0:T(8,128)} %wv_ref.1) | copy-start | bytes 1572868
  3.1 1.0 %copy-start.3 = (f32[2,256,256]{2,1,0:T(8,128)S(1)}, f32[2,256,256]{2,1,0:T(8,128)}, u32[]{:S(2)}) copy-start(f32[2,256,256]{2,1,0:T(8,128)} %wo_ref.1) | copy-start | bytes 1572868
  4.2 0.9 %copy-start.4 = (f32[1,1,256,256]{3,2,1,0:T(8,128)S(1)}, f32[1,1,256,256]{3,2,1,0:T(8,128)}, u32[]{:S(2)}) copy-start(f32[1,1,256,256]{3,2,1,0:T(8,128)} %param.5) | copy-start | bytes 786436

commit v2 on v1

--- a/solution.py
+++ b/solution.py
@@ -10,14 +10,14 @@
 D = 256
 ROWS = 256
 LAYERS = 2
-CHUNKS = 2
+CHUNKS = 4
 CROWS = ROWS // CHUNKS
 EPSILON = 1e-06
 SCORE_SHIFT = 32.0
 MESH = pl.DeviceIdType.MESH
 
 OWN, NEAR, FAR = 0, 1, 2
-NORTH, MID, SOUTH = 0, 1, 2
+PAIR, MID, AWAY = 0, 1, 2
 
 F32 = jnp.float32
 BF16 = jnp.bfloat16
@@ -53,8 +53,11 @@
     behind = gx - 2 + 4 * side
     has_onward = (onward >= 0) & (onward < nx)
     has_far = (behind >= 0) & (behind < nx)
-    has_north = gy >= 1
-    has_south = gy + 1 < ny
+    odd = lax.rem(gy, 2)
+    pair_y = gy + 1 - 2 * odd
+    away_y = gy - 1 + 2 * odd
+    seam = (gy == ny // 2) | (gy == ny // 2 - 1)
+    has_away = (away_y >= 0) & (away_y < ny)
 
     loads = [pltpu.make_async_copy(p_ref, field.at[0], load_sem.at[0])]
     for n, (src, dst) in enumerate(((wq_ref, wq), (wk_ref, wk), (wv_ref, wv), (wo_ref, wo))):
@@ -70,10 +73,10 @@
     greet(gy, partner)
     pl.when(has_onward)(lambda: greet(gy, onward))
     pl.when(has_far)(lambda: greet(gy, behind))
-    pl.when(has_north)(lambda: greet(gy - 1, gx))
-    pl.when(has_south)(lambda: greet(gy + 1, gx))
-    greetings = (1 + has_onward.astype(jnp.int32) + has_far.astype(jnp.int32)
-                 + has_north.astype(jnp.int32) + has_south.astype(jnp.int32))
+    greet(pair_y, gx)
+    pl.when(has_away)(lambda: greet(away_y, gx))
+    greetings = (2 + has_onward.astype(jnp.int32) + has_far.astype(jnp.int32)
+                 + has_away.astype(jnp.int32))
     loads[0].wait()
     pl.semaphore_wait(barrier, greetings)
 
@@ -88,21 +91,27 @@
             return field.at[layer, rows(c)]
         return halo.at[layer, slot, rows(c)]
 
-    def sends():
-        yield 0, OWN, MID, NEAR, (gy, partner), None
-        yield 1, NEAR, MID, FAR, (gy, onward), has_onward
-        for col in (OWN, NEAR, FAR):
-            there = None if col != FAR else has_far
-            yield 2 + col, col, SOUTH, col, (gy - 1, gx), has_north if there is None else has_north & there
-            yield 5 + col, col, NORTH, col, (gy + 1, gx), has_south if there is None else has_south & there
+    plain = has_away & jnp.logical_not(seam)
+    plan = [
+        (5, (MID, OWN), (AWAY, OWN), (away_y, gx), has_away),
+        (0, (MID, OWN), (MID, NEAR), (gy, partner), None),
+        (2, (MID, OWN), (PAIR, OWN), (pair_y, gx), None),
+        (1, (MID, NEAR), (MID, FAR), (gy, onward), has_onward),
+        (6, (MID, NEAR), (AWAY, NEAR), (away_y, gx), plain),
+        (3, (MID, NEAR), (PAIR, NEAR), (pair_y, gx), None),
+        (7, (MID, FAR), (AWAY, FAR), (away_y, gx), plain & has_far),
+        (4, (MID, FAR), (PAIR, FAR), (pair_y, gx), has_far),
+        (8, (AWAY, OWN), (AWAY, NEAR), (gy, partner), seam),
+        (9, (AWAY, NEAR), (AWAY, FAR), (gy, onward), seam & has_onward),
+    ]
 
     def copy(layer, send, c):
-        kind, src_col, row, col, device, _ = send
+        kind, source, target, device, _ = send
         return pltpu.make_async_remote_copy(
-            src_ref=piece(layer, MID, src_col, c, True),
-            dst_ref=piece(layer, row, col, c),
+            src_ref=piece(layer, *source, c, True),
+            dst_ref=piece(layer, *target, c),
             send_sem=send_sem.at[layer, kind, c],
-            recv_sem=recv_sem.at[layer, row * 3 + col, c],
+            recv_sem=recv_sem.at[layer, target[0] * 3 + target[1], c],
             device_id=device,
             device_id_type=MESH,
         )
@@ -113,17 +122,21 @@
         else:
             pl.when(condition)(action)
 
-    plan = list(sends())
-
-    def start(layer, src_col, c):
+    def start(layer, source, chunks):
         for send in plan:
-            if send[1] == src_col:
-                guarded(send[5], lambda send=send: copy(layer, send, c).start())
+            if send[1] == source:
+                def run(send=send):
+                    for c in chunks:
+                        copy(layer, send, c).start()
+                guarded(send[4], run)
 
     def arrival(layer, row, col, c):
-        for send in plan:
-            if send[2] == row and send[3] == col:
-                copy(layer, send, c).wait_recv()
+        there = piece(layer, row, col, c)
+        pltpu.make_async_remote_copy(
+            src_ref=there, dst_ref=there, send_sem=send_sem.at[layer, 0, c],
+            recv_sem=recv_sem.at[layer, row * 3 + col, c],
+            device_id=(gy, partner), device_id_type=MESH,
+        ).wait_recv()
 
     def process(layer, row, col):
         slot = row * 3 + col
@@ -135,19 +148,19 @@
         tot[...] += jnp.sum(weight, axis=1, keepdims=True)
         acc[...] += dot3(split(weight), tile, NN)
 
-    def await_and_process(layer, row, col):
+    def take(layer, row, col):
         def run():
             for c in range(CHUNKS + 1):
                 arrival(layer, row, col, c)
+                start(layer, (row, col), [c])
             process(layer, row, col)
-        conditions = {NORTH: has_north, SOUTH: has_south}[row]
+        condition = has_away if row == AWAY else None
         if col == FAR:
-            conditions = conditions & has_far
-        pl.when(conditions)(run)
+            condition = has_far if condition is None else condition & has_far
+        guarded(condition, run)
 
     def layer_pass(layer, carry):
-        for c in range(CHUNKS):
-            start(layer, OWN, c)
+        start(layer, (MID, OWN), range(CHUNKS))
 
         @pl.when(layer == 0)
         def _():
@@ -168,7 +181,7 @@
 
         first = lax.broadcasted_iota(jnp.int32, (8, ROWS), 0) == 0
         norms[layer, MID * 3 + OWN] = jnp.where(first, along_lanes(query), along_lanes(keys))
-        start(layer, OWN, CHUNKS)
+        start(layer, (MID, OWN), [CHUNKS])
 
         def unitize(raw):
             scale = lax.rsqrt(jnp.mean(raw * raw, axis=-1, keepdims=True) + EPSILON)
@@ -184,23 +197,14 @@
         tot[...] = jnp.zeros_like(tot)
         process(layer, MID, OWN)
 
-        for c in range(CHUNKS + 1):
-            arrival(layer, MID, NEAR, c)
-            start(layer, NEAR, c)
-        process(layer, MID, NEAR)
-        await_and_process(layer, NORTH, OWN)
-        await_and_process(layer, SOUTH, OWN)
-
-        @pl.when(has_far)
-        def _():
-            for c in range(CHUNKS + 1):
-                arrival(layer, MID, FAR, c)
-                start(layer, FAR, c)
-            process(layer, MID, FAR)
-
-        for col in (NEAR, FAR):
-            for row in (NORTH, SOUTH):
-                await_and_process(layer, row, col)
+        take(layer, MID, NEAR)
+        take(layer, PAIR, OWN)
+        take(layer, MID, FAR)
+        take(layer, AWAY, OWN)
+        take(layer, PAIR, NEAR)
+        take(layer, AWAY, NEAR)
+        take(layer, PAIR, FAR)
+        take(layer, AWAY, FAR)
 
         mean = acc[...] * (1.0 / tot[...])
         mixed = dot3(split(mean), split(wv[layer]), NN)
@@ -213,20 +217,22 @@
 
     def drain(layer, carry):
         for send in plan:
-            for c in range(CHUNKS + 1):
-                guarded(send[5], lambda send=send, c=c: copy(layer, send, c).wait_send())
+            def run(send=send):
+                for c in range(CHUNKS + 1):
+                    copy(layer, send, c).wait_send()
+            guarded(send[4], run)
         return carry
 
     lax.fori_loop(0, LAYERS, drain, 0)
 
 
 def on_device(ny, nx, patches, w_query, w_key, w_value, w_out):
-    any_space = pl.BlockSpec(memory_space=pl.ANY)
+    in_hbm = pl.BlockSpec(memory_space=pltpu.HBM)
     weight = pltpu.VMEM((LAYERS, D, D), F32)
     out = pl.pallas_call(
         functools.partial(kernel, ny, nx),
         out_shape=jax.ShapeDtypeStruct((ROWS, D), F32),
-        in_specs=[any_space] * 5,
+        in_specs=[in_hbm] * 5,
         out_specs=pl.BlockSpec(memory_space=pltpu.VMEM),
         scratch_shapes=[
             pltpu.VMEM((LAYERS + 1, ROWS, D), F32),
@@ -237,12 +243,12 @@
             pltpu.VMEM((2 * ROWS, D), BF16),
             pltpu.VMEM((ROWS, D), F32),
             pltpu.VMEM((ROWS, 1), F32),
-            pltpu.SemaphoreType.DMA((LAYERS, 8, CHUNKS + 1)),
+            pltpu.SemaphoreType.DMA((LAYERS, 10, CHUNKS + 1)),
             pltpu.SemaphoreType.DMA((LAYERS, 9, CHUNKS + 1)),
             pltpu.SemaphoreType.DMA((5,)),
         ],
         compiler_params=pltpu.CompilerParams(
-            collective_id=0, has_side_effects=True, vmem_limit_bytes=48 * 1024 * 1024
+            collective_id=0, has_side_effects=True, vmem_limit_bytes=67043328
         ),
     )(patches[0, 0], w_query, w_key, w_value, w_out)
     return out[None, None]

time: 58.6 us -> 52.5 us (0.90)
  the two profiles are of different devices: /device:TPU:136 before, /device:TPU:198 now
where the time goes in v2:
time: 52.5 us; the launch traced here: 52.3 us
  Pallas kernels  50.6 us (96%)
  local copies, waits for them, and re-layouts  1.67 us (3%)
    pallas_call x1, Pallas kernels, on_device(): pl.pallas_call(functools.partial(kernel, ny, nx), out_shape=jax.ShapeDtyp...  50.6 us
    unnamed x1, local copies, waits for them, and re-layouts  1.67 us

profile of v2, /device:TPU:198, one launch (start us, length us, event | category | flops | bytes accessed | tf_op | source)
XLA Modules:
  0.0 52.3 jit_solution(18350125268898951333)
XLA Ops:
  0.0 50.6 %shard_map.55 = f32[256,256]{1,0:T(8,128)} custom-call(f32[256,256]{1,0:T(8,128)} %bitcast.3, f32[2,256,256]{2,1,0:T(8,128)} %wq_ref.1, f32[2,256,256]{2,1,0:T(8,128)} %wk_ref.1, f32[2,256,256]{2,1,0:T(8,128)} %wv_ref.1, f32[2,256,256]{2,1,0:T(8,128)} %wo_ref.1), custom_call_target="tpu_custom_call" | custom-call | tf_op jit(solution)/shard_map/pallas_call | solution.py:232
  50.6 1.7 %copy.7 = f32[1,1,256,256]{3,2,1,0:T(8,128)} copy(f32[1,1,256,256]{3,2,1,0:T(8,128)} %bitcast.2) | data formatting | bytes 524288

commit v3 on v2

--- a/solution.py
+++ b/solution.py
@@ -62,8 +62,7 @@
     loads = [pltpu.make_async_copy(p_ref, field.at[0], load_sem.at[0])]
     for n, (src, dst) in enumerate(((wq_ref, wq), (wk_ref, wk), (wv_ref, wv), (wo_ref, wo))):
         loads.append(pltpu.make_async_copy(src, dst, load_sem.at[n + 1]))
-    for load in loads:
-        load.start()
+    loads[0].start()
 
     barrier = pltpu.get_barrier_semaphore()
 
@@ -78,6 +77,8 @@
     greetings = (2 + has_onward.astype(jnp.int32) + has_far.astype(jnp.int32)
                  + has_away.astype(jnp.int32))
     loads[0].wait()
+    for load in loads[1:]:
+        load.start()
     pl.semaphore_wait(barrier, greetings)
 
     def rows(c):
@@ -200,8 +201,8 @@
         take(layer, MID, NEAR)
         take(layer, PAIR, OWN)
         take(layer, MID, FAR)
+        take(layer, PAIR, NEAR)
         take(layer, AWAY, OWN)
-        take(layer, PAIR, NEAR)
         take(layer, AWAY, NEAR)
         take(layer, PAIR, FAR)
         take(layer, AWAY, FAR)

time: 52.5 us -> 54.4 us (1.036)
  Pallas kernels: 50.6 us -> 52.6 us
    pallas_call x1, Pallas kernels: 50.6 us -> 52.6 us  [on_device(): pl.pallas_call(functools.partial(kernel, ny, nx), out_shape=jax.ShapeDtyp...]
where the time goes in v3:
time: 54.4 us; the launch traced here: 54.2 us
  Pallas kernels  52.6 us (97%)
  local copies, waits for them, and re-layouts  1.67 us (3%)
    pallas_call x1, Pallas kernels, on_device(): pl.pallas_call(functools.partial(kernel, ny, nx), out_shape=jax.ShapeDtyp...  52.6 us
    unnamed x1, local copies, waits for them, and re-layouts  1.67 us

profile of v3, /device:TPU:198, one launch (start us, length us, event | category | flops | bytes accessed | tf_op | source)
XLA Modules:
  0.0 54.2 jit_solution(9199863835294738680)
XLA Ops:
  0.0 52.6 %shard_map.55 = f32[256,256]{1,0:T(8,128)} custom-call(f32[256,256]{1,0:T(8,128)} %bitcast.3, f32[2,256,256]{2,1,0:T(8,128)} %wq_ref.1, f32[2,256,256]{2,1,0:T(8,128)} %wk_ref.1, f32[2,256,256]{2,1,0:T(8,128)} %wv_ref.1, f32[2,256,256]{2,1,0:T(8,128)} %wo_ref.1), custom_call_target="tpu_custom_call" | custom-call | tf_op jit(solution)/shard_map/pallas_call | solution.py:233
  52.6 1.7 %copy.7 = f32[1,1,256,256]{3,2,1,0:T(8,128)} copy(f32[1,1,256,256]{3,2,1,0:T(8,128)} %bitcast.2) | data formatting | bytes 524288
